TPU v7x, 128 devices: a whole 4x4x4 slice. The times are simulated.
128 devices in a mesh: row: 4 (over x), col: 8 (over z_lo, y), layer: 4 (over z_hi, core).
Axes of the slice: x: 4, y: 4, z: 4 (z_hi: 2, z_lo: 2; z = z_hi * 2 + z_lo), core: 2. Of those that a mesh axis runs over, the one named last changes fastest.
Arguments:
- a_blocks: float32 [4096, 4096], P('row', ('col', 'layer')), may hold values from -6 to 6
- mask_a: int32 [64, 64], P('row', ('col', 'layer')), may hold values from 0 to 1, as said below
- b_blocks: float32 [4096, 32768], P('row', ('col', 'layer')), may hold values from -0.25 to 0.25
- mask_b: int32 [64, 512], P('row', ('col', 'layer')), may hold values from 0 to 1
Outputs:
- product: float32 [4096, 32768], P('row', ('col', 'layer'))
Inputs may be any that keep to these rules, and one draw needn't show every extreme that they name: Within one device's shard of mask_a (16 block rows by 2 inner block indices) at most 8 blocks are stored; the shard of the first 16 block rows and first 2 inner indices stores exactly 8.
All inputs are finite; a program needn't handle non-finite values.
Results may differ from a plain program's by a relative error of at most 0.00007.
Values sent between devices are 32-bit elements; how exact they have to be, the bound alone decides.
No kernel may reach another device: no remote copies, remote signals or barrier semaphores. Data moves between devices by JAX's collectives and lax.ppermute only.
A program may use at most 128 MiB of HBM per device.

v0:
```python
import jax
import jax.numpy as jnp
from jax import lax
from jax.sharding import PartitionSpec as P

BLOCK = 64


def expand(mask):
    return jnp.repeat(jnp.repeat(mask, BLOCK, axis=0), BLOCK, axis=1).astype(jnp.float32)


def shards(a_blocks, mask_a, b_blocks, mask_b):
    b_masked = b_blocks * expand(mask_b)
    b_whole = lax.all_gather(b_masked, "row", axis=0, tiled=True)
    a_masked = a_blocks * expand(mask_a)
    return jnp.dot(
        lax.all_gather(a_masked, ("col", "layer"), axis=1, tiled=True),
        b_whole,
        precision=lax.Precision.HIGHEST,
        preferred_element_type=jnp.float32,
    )


def solution(mesh):
    placed = (
        P("row", ("col", "layer")),
        P("row", ("col", "layer")),
        P("row", ("col", "layer")),
        P("row", ("col", "layer")),
    )
    return jax.shard_map(
        shards, mesh=mesh, in_specs=placed, out_specs=P("row", ("col", "layer")), check_vma=False
    )
```

profile of v0, /device:TPU:1, one launch (start us, length us, event | category | flops | bytes accessed | tf_op | source)
XLA Modules:
  0.0 392.4 jit_solution(702926884030204920)
XLA Ops:
  6.5 0.0 copy-start
  6.5 0.0 copy-start.1
  6.5 0.0 all-gather.5.cloned.1.call-start
  6.5 5.4 %copy.8 = f32[1024,1024]{0,1:T(8,128)} copy(f32[1024,1024]{1,0:T(8,128)} %param.6) | data formatting | bytes 8388608 | tf_op args[2]
  11.9 0.7 convert_element_type.25
  12.6 0.1 copy.7
  12.7 0.1 broadcast_in_dim.14
  12.8 0.1 convert_element_type.26
  12.9 5.1 %bitcast_multiply_fusion = f32[1024,1024]{0,1:T(8,128)} fusion(f32[1024,1024]{0,1:T(8,128)} %copy.8, f32[1024,16]{0,1:T(8,128)S(1)} %convert_element_type.26), kind=kLoop, calls=%fused_computation | loop fusion | flops 1048576 | bytes 8454144 | tf_op jit(solution)/shard_map/mul | solution.py:14
  18.0 0.0 all-gather.5.cloned.1.call-update
  18.0 0.0 all-gather.3.cloned.1.call-start
  18.0 0.0 copy-done
  18.1 0.2 copy.6
  18.3 0.0 copy-done.1
  18.3 0.1 broadcast_in_dim.12
  18.4 0.1 convert_element_type.23
  18.4 0.9 bitcast_multiply_fusion.1
  19.3 0.0 all-gather.3.cloned.1.call-update
  19.3 156.1 %all-gather.5.cloned.1.call-done = f32[4096,1024]{0,1:T(8,128)} async-done(((f32[1024,1024]{0,1:T(8,128)}), f32[4096,1024]{0,1:T(8,128)}) %all-gather.5.cloned.1.call-update) | async-done | bytes 16777232 | tf_op jit(solution)/shard_map/all_gather | solution.py:15
  175.4 100.4 %all-gather.3.cloned.1.call-done = f32[1024,4096]{0,1:T(8,128)} async-done(((f32[1024,128]{0,1:T(8,128)}), f32[1024,4096]{0,1:T(8,128)}) %all-gather.3.cloned.1.call-update) | async-done | bytes 16777232 | tf_op jit(solution)/shard_map/all_gather | solution.py:18
  275.8 109.8 %fusion = f32[1024,1024]{1,0:T(8,128)} fusion(f32[1024,4096]{0,1:T(8,128)} %all-gather.3.cloned.1.call-done, f32[4096,1024]{0,1:T(8,128)} %all-gather.5.cloned.1.call-done), kind=kOutput, calls=%fused_computation.2 | convolution fusion | flops 51539607552 | bytes 37748736 | tf_op jit(solution)/shard_map/dot_general | solution.py:17
  (1 shorter events, 0.0 us)
Async XLA Ops:
  6.5 11.5 %copy-start = (f32[1024,128]{1,0:T(8,128)S(1)}, f32[1024,128]{1,0:T(8,128)}, u32[]{:S(2)}) copy-start(f32[1024,128]{1,0:T(8,128)} %param.4) | copy-start | bytes 1572868
  6.5 11.7 %copy-start.1 = (s32[16,2]{0,1:T(2,128)S(1)}, s32[16,2]{0,1:T(2,128)}, u32[]{:S(2)}) copy-start(s32[16,2]{0,1:T(2,128)} %param.5) | copy-start | bytes 388
  6.5 168.9 %all-gather.5.cloned.1.call-start = ((), (), s32[]{:S(2)}) async-start(), calls=%async_computation.1 | async-start | bytes 20971520 | tf_op jit(solution)/shard_map/all_gather | solution.py:15
  18.0 257.8 %all-gather.3.cloned.1.call-start = ((), (), s32[]{:S(2)}) async-start(), calls=%async_computation | async-start | bytes 17301504 | tf_op jit(solution)/shard_map/all_gather | solution.py:18
Sparse Core Ops, SparseCore 0:
  18.1 157.2 all-gather.4
  177.1 98.6 all-gather.2
where the time goes:
time: 393 us; the launch traced here: 392 us
  waiting for transfers between devices  256 us (65%)
  matrix products  110 us (28%)
  between operations  13.4 us (3%)
  other arithmetic  6.62 us (2%)
  local copies, waits for them, and re-layouts  6.02 us (2%)
    all_gather x1, waiting for transfers between devices, shards(): b_whole = lax.all_gather(b_masked, 'row', axis=0, tiled=True)  156 us
    dot_general x1, matrix products, shards(): jnp.dot(lax.all_gather(a_masked, ('col', 'layer'), axis=1, tiled=True), b...  110 us
    all_gather x1, waiting for transfers between devices, shards(): lax.all_gather(a_masked, ('col', 'layer'), axis=1, tiled=True)  100 us
  transfers between devices with their start and end apart: 2, of which 2 were waited for; matrix products, arithmetic and copies ran while one was open for 0% of the time, Pallas kernels for 0%

commit v1 on v0

--- a/solution.py
+++ b/solution.py
@@ -11,8 +11,35 @@
 
 
 def shards(a_blocks, mask_a, b_blocks, mask_b):
+
+    def region_solve(sample, axis_id, array_dim):
+        t_next = jax.lax.axis_size(axis_id)
+        kept_arr, val2, local_out = (t_next, jax.lax.axis_index(axis_id), sample.shape[array_dim])
+        samples = [
+            d * kept_arr if hop_no == array_dim else d for hop_no, d in enumerate(sample.shape)
+        ]
+        res = jnp.zeros(samples, sample.dtype)
+        small = upper = sample
+        carry_out = lax.dynamic_update_slice_in_dim(res, sample, val2 * local_out, axis=array_dim)
+        for u in range(1, kept_arr // 2 + 1):
+            current_value = range(kept_arr)
+            vec_out = list(map(lambda hop_no: (hop_no, (hop_no + 1) % kept_arr), current_value))
+            small = jax.lax.ppermute(small, axis_name=axis_id, perm=vec_out)
+            carry_out = lax.dynamic_update_slice_in_dim(
+                carry_out, small, (val2 - u) % kept_arr * local_out, axis=array_dim
+            )
+            if 2 * u < kept_arr:
+                arr_now = list(
+                    map(lambda hop_no: (hop_no, (hop_no - 1) % kept_arr), range(kept_arr))
+                )
+                upper = jax.lax.ppermute(upper, axis_name=axis_id, perm=arr_now)
+                carry_out = lax.dynamic_update_slice_in_dim(
+                    carry_out, upper, (val2 + u) % kept_arr * local_out, axis=array_dim
+                )
+        return carry_out
+
     b_masked = b_blocks * expand(mask_b)
-    b_whole = lax.all_gather(b_masked, "row", axis=0, tiled=True)
+    b_whole = region_solve(b_masked, "row", 0)
     a_masked = a_blocks * expand(mask_a)
     return jnp.dot(
         lax.all_gather(a_masked, ("col", "layer"), axis=1, tiled=True),

time: 393 us -> 337 us (0.86)
  waiting for transfers between devices: 256 us -> 172 us
  local copies, waits for them, and re-layouts: 6.02 us -> 29.1 us
    ppermute x0 -> x3, waiting for transfers between devices: none -> 172 us  [the longest x2 172 us: region_solve(): small = jax.lax.ppermute(small, axis_name=axis_id, perm=vec_out)]
    all_gather x1 -> x0, waiting for transfers between devices: 156 us -> none  [shards(): b_whole = lax.all_gather(b_masked, 'row', axis=0, tiled=True)]
    all_gather x1, waiting for transfers between devices: 100 us -> 0.01 us  [shards(): lax.all_gather(a_masked, ('col', 'layer'), axis=1, tiled=True)]
    dynamic_update_slice x0 -> x3, local copies, waits for them, and re-layouts: none -> 14.1 us  [the longest x2 9.44 us: region_solve(): lax.dynamic_update_slice_in_dim(carry_out, small, (val2 - u) % kept_arr *...]
    broadcast_in_dim x0 -> x1, local copies, waits for them, and re-layouts: none -> 8 us  [region_solve(): res = jnp.zeros(samples, sample.dtype)]
    mul x1 -> x0, other arithmetic: 5.06 us -> none  [shards(): b_masked = b_blocks * expand(mask_b)]
    dynamic_update_slice x0 -> x1, other arithmetic: none -> 4.36 us  [region_solve(): lax.dynamic_update_slice_in_dim(res, sample, val2 * local_out, axis=array...]
  transfers between devices with their start and end apart: 2 -> 4, of which waited for: 2 -> 2; matrix products, arithmetic and copies ran while one was open for 0% -> 10% of each run, Pallas kernels for 0% -> 0%
where the time goes in v1:
time: 337 us; the launch traced here: 335 us
  waiting for transfers between devices  172 us (51%)
  matrix products  110 us (33%)
  local copies, waits for them, and re-layouts  29.1 us (9%)
  between operations  13.4 us (4%)
  other arithmetic  6.59 us (2%)
  starting transfers between devices  3.6 us (1%)
    ppermute x2, waiting for transfers between devices, region_solve(): small = jax.lax.ppermute(small, axis_name=axis_id, perm=vec_out)  172 us
    dot_general x1, matrix products, shards(): jnp.dot(lax.all_gather(a_masked, ('col', 'layer'), axis=1, tiled=True), b...  110 us
    dynamic_update_slice x2, local copies, waits for them, and re-layouts, region_solve(): lax.dynamic_update_slice_in_dim(carry_out, small, (val2 - u) % kept_arr *...  9.44 us
    broadcast_in_dim x1, local copies, waits for them, and re-layouts, region_solve(): res = jnp.zeros(samples, sample.dtype)  8 us
  transfers between devices with their start and end apart: 4, of which 2 were waited for; matrix products, arithmetic and copies ran while one was open for 10% of the time, Pallas kernels for 0%

profile of v1, /device:TPU:1, one launch (start us, length us, event | category | flops | bytes accessed | tf_op | source)
XLA Modules:
  0.0 335.0 jit_solution(9454907571476307550)
XLA Ops:
  6.5 0.0 all-gather.2.cloned.1.call-start
  6.5 1.2 copy.6
  7.8 0.7 convert_element_type.22
  8.5 0.1 broadcast_in_dim.15
  8.5 0.1 convert_element_type.23
  8.6 0.9 bitcast_multiply_fusion.1
  9.5 0.0 all-gather.2.cloned.1.call-update
  9.5 5.3 %copy.8 = f32[1024,1024]{0,1:T(8,128)} copy(f32[1024,1024]{1,0:T(8,128)} %param.6) | data formatting | bytes 8388608 | tf_op args[2]
  14.9 0.7 convert_element_type.25
  15.5 0.1 copy.7
  15.6 0.1 broadcast_in_dim.18
  15.7 0.1 convert_element_type.26
  15.8 0.0 copy-start
  15.8 8.0 %broadcast_in_dim.17 = f32[4096,1024]{0,1:T(8,128)} broadcast(f32[]{:T(128)} %constant.30.clone.1), dimensions={} | broadcast | bytes 16777220 | tf_op jit(solution)/shard_map/broadcast_in_dim | solution.py:21
  23.8 0.0 copy-done
  23.8 4.4 %constant_dynamic-update-slice_fusion.3 = (f32[4096,1024]{0,1:T(8,128)}, f32[1024,1024]{0,1:T(8,128)}) fusion(f32[4096,1024]{0,1:T(8,128)} %broadcast_in_dim.17, s32[]{:T(128)S(6)} %select_n.27, f32[1024,1024]{0,1:T(8,128)S(1)} %copy-done, f32[1024,16]{0,1:T(8,128)S(1)} %convert_element_type.26), kind=kLoop, calls=%fused_computation.5 | loop fusion | flops 1048576 | bytes 12648452 | tf_op jit(solution)/shard_map/dynamic_update_slice | solution.py:23
  28.2 2.0 collective-permute-start
  30.2 1.3 collective-permute-start.1
  31.5 90.2 %collective-permute-done = f32[1024,1024]{0,1:T(8,128)} collective-permute-done((f32[1024,1024]{0,1:T(8,128)}, f32[1024,1024]{0,1:T(8,128)}, u32[]{:S(2)}, u32[]{:S(2)}) %collective-permute-start) | collective-permute-done | bytes 4194336 | tf_op jit(solution)/shard_map/ppermute | solution.py:27
  121.7 0.2 collective-permute-start.2
  122.0 4.8 %constant_dynamic-update-slice_fusion.2 = f32[4096,1024]{0,1:T(8,128)} fusion(f32[4096,1024]{0,1:T(8,128)} %get-tuple-element.5, f32[1024,1024]{0,1:T(8,128)} %collective-permute-done, s32[]{:T(128)S(6)} %select_n.29), kind=kLoop, calls=%fused_computation.4 | loop fusion | bytes 8388612 | tf_op jit(solution)/shard_map/dynamic_update_slice | solution.py:28
  126.7 0.0 collective-permute-done.1
  126.7 4.7 %constant_dynamic-update-slice_fusion.1 = f32[4096,1024]{0,1:T(8,128)} fusion(f32[4096,1024]{0,1:T(8,128)} %constant_dynamic-update-slice_fusion.2, f32[1024,1024]{0,1:T(8,128)} %collective-permute-done.1, s32[]{:T(128)S(6)} %select_n.31), kind=kLoop, calls=%fused_computation.3 | loop fusion | bytes 8388612 | tf_op jit(solution)/shard_map/dynamic_update_slice | solution.py:36
  131.4 82.3 %collective-permute-done.2 = f32[1024,1024]{0,1:T(8,128)} collective-permute-done((f32[1024,1024]{0,1:T(8,128)}, f32[1024,1024]{0,1:T(8,128)}, u32[]{:S(2)}, u32[]{:S(2)}) %collective-permute-start.2) | collective-permute-done | bytes 4194336 | tf_op jit(solution)/shard_map/ppermute | solution.py:27
  213.7 4.7 %constant_dynamic-update-slice_fusion = f32[4096,1024]{0,1:T(8,128)} fusion(f32[4096,1024]{0,1:T(8,128)} %constant_dynamic-update-slice_fusion.1, f32[1024,1024]{0,1:T(8,128)} %collective-permute-done.2, s32[]{:T(128)S(6)} %select_n.33), kind=kLoop, calls=%fused_computation.2 | loop fusion | bytes 8388612 | tf_op jit(solution)/shard_map/dynamic_update_slice | solution.py:28
  218.4 0.0 all-gather.2.cloned.1.call-done
  218.4 109.8 %fusion = f32[1024,1024]{1,0:T(8,128)} fusion(f32[1024,4096]{0,1:T(8,128)} %all-gather.2.cloned.1.call-done, f32[4096,1024]{0,1:T(8,128)} %constant_dynamic-update-slice_fusion), kind=kOutput, calls=%fused_computation.6 | convolution fusion | flops 51539607552 | bytes 37748736 | tf_op jit(solution)/shard_map/dot_general | solution.py:44
Async XLA Ops:
  6.5 211.9 %all-gather.2.cloned.1.call-start = ((), (), s32[]{:S(2)}) async-start(), calls=%async_computation | async-start | bytes 17301504 | tf_op jit(solution)/shard_map/all_gather | solution.py:45
  15.8 8.0 %copy-start = (f32[1024,1024]{0,1:T(8,128)S(1)}, f32[1024,1024]{0,1:T(8,128)}, u32[]{:S(2)}) copy-start(f32[1024,1024]{0,1:T(8,128)} %copy.8) | copy-start | bytes 12582916
  28.2 93.5 %collective-permute-start = (f32[1024,1024]{0,1:T(8,128)}, f32[1024,1024]{0,1:T(8,128)}, u32[]{:S(2)}, u32[]{:S(2)}) collective-permute-start(f32[1024,1024]{0,1:T(8,128)} %get-tuple-element.6), channel_id=1, source_target_pairs={{0,32},{32,64},{64,96},{96,0},{1,33},{33,65},{65,97},{97,1},{2,34}... | collective-permute-start | bytes 12582920 | tf_op jit(solution)/shard_map/ppermute | solution.py:27
  30.2 96.5 %collective-permute-start.1 = (f32[1024,1024]{0,1:T(8,128)}, f32[1024,1024]{0,1:T(8,128)}, u32[]{:S(2)}, u32[]{:S(2)}) collective-permute-start(f32[1024,1024]{0,1:T(8,128)} %get-tuple-element.6), channel_id=1, source_target_pairs={{0,96},{32,0},{64,32},{96,64},{1,97},{33,1},{65,33},{97,65},{2,98}... | collective-permute-start | bytes 12582920 | tf_op jit(solution)/shard_map/ppermute | solution.py:35
  121.7 92.0 %collective-permute-start.2 = (f32[1024,1024]{0,1:T(8,128)}, f32[1024,1024]{0,1:T(8,128)}, u32[]{:S(2)}, u32[]{:S(2)}) collective-permute-start(f32[1024,1024]{0,1:T(8,128)} %collective-permute-done), channel_id=1, source_target_pairs={{0,32},{32,64},{64,96},{96,0},{1,33},{33,65},{65,97},{97,1},{2,34}... | collective-permute-start | bytes 12582920 | tf_op jit(solution)/shard_map/ppermute | solution.py:27
Sparse Core Ops, SparseCore 0:
  9.6 100.8 all-gather.1
